TPU v7x, 256 devices: a whole 4x4x8 slice. The times are simulated.
256 devices in a mesh: tile: 64 (over y, z, core), sec: 4 (over x).
Axes of the slice: x: 4, y: 4, z: 8, core: 2. Of those that a mesh axis runs over, the one named last changes fastest.
Arguments:
- voltage: float32 [8192, 512], P('tile', 'sec'), may hold values from -6 to 6
- conductance: float32 [8192, 512], P('tile', 'sec'), may hold values from 0.2 to 2
- reversal: float32 [8192, 512], P('tile', 'sec'), may hold values from -1 to 1
- drive: bfloat16 [8, 8192, 512], P(None, 'tile', 'sec'), may hold values from -6 to 6
- inv_cable: float32 [128, 128], replicated, may hold values from -1 to 1
- owner_map: int32 [8192], P('tile'), may hold values from 0 to 63, as said below
- peer_counts: int32 [64, 64], P('tile'), may hold values from 0 to 4, as said below
- pattern: int32 [4, 8192, 2], P('sec', 'tile'), may hold values from 0 to 31, all different within a row
- transfer: bfloat16 [4, 8192, 2, 128, 128], P('sec', 'tile'), may hold values from -0.01171875 to 0.01171875
Outputs:
- final_voltage: float32 [8192, 512], P('tile', 'sec')
- probe: float32 [8, 4096], P(None, ('tile', 'sec'))
Inputs may be any that keep to these rules, and one draw needn't show every extreme that they name: `owner_map`: every depth tile owns exactly 128 cells; the cells c with c // 128 = u include at most 4 cells of one owner, and exactly 4 of some owner. peer_counts[d, u] is the number of cells c with c // 128 = u and owner_map[c] = d. `pattern`: the 2 contact tiles of one slot and section differ.
All inputs are finite; a program needn't handle non-finite values.
Results may differ from a plain program's by a relative error of at most 0.0029.
Values may be sent and summed in bfloat16 or wider, within the bound.
A program may use at most 64 MiB of HBM per device.

v0:
```python
import jax
import jax.numpy as jnp
from jax import lax
from jax.sharding import PartitionSpec as P

CONTACTS = 4096
TIME_STEP = 0.25
AXIAL = 2.0


def padded_2(block, sides, width):
    for axis, dim in sides:
        count = lax.axis_size(axis)
        forward = [(i, i + 1) for i in range(count - 1)]
        backward = [(target, source) for source, target in forward]
        low = lax.ppermute(
            lax.slice_in_dim(block, block.shape[dim] - width, None, axis=dim), axis, forward
        )
        high = lax.ppermute(lax.slice_in_dim(block, 0, width, axis=dim), axis, backward)
        block = jnp.concatenate([low, block, high], axis=dim)
    return block


def cable_update(voltage_now, conductance, reversal, drive_now, inv_cable):
    padded = padded_2(voltage_now.astype(jnp.bfloat16), (("sec", 1),), 1).astype(voltage_now.dtype)
    columns = jnp.arange(voltage_now.shape[1], dtype=jnp.int32)
    first_col = (columns == 0).astype(jnp.float32)
    last_col = (columns == voltage_now.shape[1] - 1).astype(jnp.float32)
    boundary = first_col * (padded[:, :-2] - voltage_now) + last_col * (padded[:, 2:] - voltage_now)
    driven = drive_now.astype(jnp.float32)
    right_side = voltage_now * (1.0 - TIME_STEP * conductance) + TIME_STEP * (
        conductance * reversal + driven + AXIAL * boundary
    )
    voltage_next = jnp.einsum("ci,ji->cj", right_side, inv_cable, precision=lax.Precision.HIGHEST)
    current = (conductance * (voltage_next - reversal) - driven).astype(jnp.bfloat16)
    return (voltage_next, current)


def on_device(
    voltage, conductance, reversal, drive, inv_cable, owner_map, peer_counts, pattern, transfer
):
    cell_count = voltage.shape[0]
    seg_width = voltage.shape[1]
    step_count = drive.shape[0]
    tile_count = lax.axis_size("tile")
    section_count = lax.axis_size("sec")
    capacity = 2 * cell_count // tile_count
    owners = jnp.arange(tile_count, dtype=jnp.int32)
    member = (owner_map[:, None] == owners[None, :]).astype(jnp.int32)
    rank_within = jnp.sum(jnp.cumsum(member, axis=0) * member, axis=1) - 1
    placed = owner_map * capacity + rank_within
    source_row = (
        jnp.full((tile_count * capacity,), cell_count, jnp.int32)
        .at[placed]
        .set(jnp.arange(cell_count, dtype=jnp.int32))
    )
    blank_row = jnp.zeros((1, seg_width), jnp.bfloat16)

    def advance_send(voltage_now, drive_now):
        voltage_next, current = cable_update(
            voltage_now, conductance, reversal, drive_now, inv_cable
        )
        outgoing = jnp.take(jnp.concatenate([current, blank_row], axis=0), source_row, axis=0)
        outgoing = outgoing.reshape(tile_count, capacity, seg_width)
        arrived = lax.all_to_all(outgoing, "tile", split_axis=0, concat_axis=0, tiled=True)
        return (voltage_next, arrived)

    final_voltage, arrived = lax.scan(advance_send, voltage, drive)
    received = arrived.reshape(step_count, tile_count * capacity, seg_width)
    counts = peer_counts[0]
    end_rows = jnp.cumsum(counts)
    starts = end_rows - counts
    slot_ids = jnp.arange(cell_count, dtype=jnp.int32)
    source = jnp.sum((end_rows[None, :] <= slot_ids[:, None]).astype(jnp.int32), axis=1)
    offset = jnp.sum(jnp.where(source[:, None] == owners[None, :], starts[None, :], 0), axis=1)
    gather_rows = source * capacity + slot_ids - offset
    ordered = jnp.take(received, gather_rows, axis=1)
    weights = transfer[0]
    layout = pattern[0]
    contact_width = weights.shape[3]
    tile_total = CONTACTS // contact_width
    tile_sums = jnp.einsum("tsi,skic->tskc", ordered, weights, preferred_element_type=jnp.float32)
    select = (layout[:, :, None] == jnp.arange(tile_total, dtype=jnp.int32)[None, None, :]).astype(
        jnp.float32
    )
    partial_sum = jnp.einsum("tskc,skq->tqc", tile_sums, select, precision=lax.Precision.HIGHEST)
    partial_sum = partial_sum.reshape(step_count, tile_total * contact_width)
    summed = lax.psum(partial_sum, ("tile", "sec"))
    share_width = summed.shape[1] // (tile_count * section_count)
    position = lax.axis_index("tile") * section_count + lax.axis_index("sec")
    probe_share = lax.dynamic_slice_in_dim(summed, position * share_width, share_width, 1)
    return (final_voltage, probe_share)


def solution(mesh):
    placed = (
        P("tile", "sec"),
        P("tile", "sec"),
        P("tile", "sec"),
        P(None, "tile", "sec"),
        P(),
        P("tile"),
        P("tile", None),
        P("sec", "tile", None),
        P("sec", "tile", None, None, None),
    )
    return jax.shard_map(
        on_device,
        mesh=mesh,
        in_specs=placed,
        out_specs=(P("tile", "sec"), P(None, ("tile", "sec"))),
        check_vma=False,
    )
```

profile of v0, /device:TPU:8, one launch (start us, length us, event | category | flops | bytes accessed | tf_op | source)
XLA Modules:
  0.0 478.0 jit_solution(9085325909894427495)
XLA Ops:
  14.3 208.3 %while.13 = (s32[]{:T(128)}, f32[128,128]{1,0:T(8,128)S(1)}, bf16[8,64,4,128]{3,2,1,0:T(4,128)(2,1)S(1)}, f32[128,128]{1,0:T(8,128)}, bf16[8,128,128]{2,1,0:T(8,...) while((s32[]{:T(128)}, f32[128,128]{1,0:T(8,128)S(1)}, ...), condition=%wide.region_4.5_spmd, body=%wide.region_3.4_spmd.sunk | while | flops 25629952 | bytes 1626603 | solution.py:68
  14.4 1.3 collective-permute-start
  15.7 4.5 collective-permute-start.1
  20.4 1.4 collective-permute-done.1
  21.9 1.3 fusion.52
  24.8 12.1 %all-to-all-start = ((bf16[64,4,128]{2,1,0:T(4,128)(2,1)}), bf16[64,4,128]{2,1,0:T(4,128)(2,1)S(1)}, u32[]{:S(2)}, u32[]{:S(2)}) async-start(bf16[64,4,128]{2,1,0:T(4,128)(2,1)} %broadcast_select_fusion.2), calls=%async_computation | async-start | bytes 131072 | tf_op jit(solution)/shard_map/while/body/eval_jaxpr/all_to_all | solution.py:65
  36.9 8.8 %all-to-all-done = bf16[64,4,128]{2,1,0:T(4,128)(2,1)S(1)} async-done(((bf16[64,4,128]{2,1,0:T(4,128)(2,1)}), bf16[64,4,128]{2,1,0:T(4,128)(2,1)S(1)}, u32[]{:S(2)}, u32[]{:S(2)}) %all-to-all-start) | async-done | bytes 65568 | tf_op jit(solution)/shard_map/while/body/eval_jaxpr/all_to_all | solution.py:65
  45.9 1.3 collective-permute-start
  47.2 4.9 %collective-permute-start.1 = (bf16[128,1]{1,0:T(8,128)(2,1)S(1)}, bf16[128,1]{1,0:T(8,128)(2,1)S(1)}, u32[]{:S(2)}, u32[]{:S(2)}) collective-permute-start(bf16[128,1]{1,0:T(8,128)(2,1)S(1)} %get-tuple-element.171), channel_id=1, source_target_pairs={{0,1},{1,2},{2,3},{4,5},{5,6},{6,7},{8,9},{9,10},{10,11},{12,13},{... | collective-permute-start | bytes 776 | tf_op jit(solution)/shard_map/while/body/eval_jaxpr/ppermute | solution.py:16
  52.2 1.4 collective-permute-done.1
  53.7 1.3 fusion.52
  56.7 5.5 %all-to-all-start = ((bf16[64,4,128]{2,1,0:T(4,128)(2,1)}), bf16[64,4,128]{2,1,0:T(4,128)(2,1)S(1)}, u32[]{:S(2)}, u32[]{:S(2)}) async-start(bf16[64,4,128]{2,1,0:T(4,128)(2,1)} %broadcast_select_fusion.2), calls=%async_computation | async-start | bytes 131072 | tf_op jit(solution)/shard_map/while/body/eval_jaxpr/all_to_all | solution.py:65
  62.2 8.8 %all-to-all-done = bf16[64,4,128]{2,1,0:T(4,128)(2,1)S(1)} async-done(((bf16[64,4,128]{2,1,0:T(4,128)(2,1)}), bf16[64,4,128]{2,1,0:T(4,128)(2,1)S(1)}, u32[]{:S(2)}, u32[]{:S(2)}) %all-to-all-start) | async-done | bytes 65568 | tf_op jit(solution)/shard_map/while/body/eval_jaxpr/all_to_all | solution.py:65
  71.2 1.3 collective-permute-start
  72.5 4.9 %collective-permute-start.1 = (bf16[128,1]{1,0:T(8,128)(2,1)S(1)}, bf16[128,1]{1,0:T(8,128)(2,1)S(1)}, u32[]{:S(2)}, u32[]{:S(2)}) collective-permute-start(bf16[128,1]{1,0:T(8,128)(2,1)S(1)} %get-tuple-element.171), channel_id=1, source_target_pairs={{0,1},{1,2},{2,3},{4,5},{5,6},{6,7},{8,9},{9,10},{10,11},{12,13},{... | collective-permute-start | bytes 776 | tf_op jit(solution)/shard_map/while/body/eval_jaxpr/ppermute | solution.py:16
  77.5 1.4 collective-permute-done.1
  79.0 1.3 fusion.52
  81.9 5.5 %all-to-all-start = ((bf16[64,4,128]{2,1,0:T(4,128)(2,1)}), bf16[64,4,128]{2,1,0:T(4,128)(2,1)S(1)}, u32[]{:S(2)}, u32[]{:S(2)}) async-start(bf16[64,4,128]{2,1,0:T(4,128)(2,1)} %broadcast_select_fusion.2), calls=%async_computation | async-start | bytes 131072 | tf_op jit(solution)/shard_map/while/body/eval_jaxpr/all_to_all | solution.py:65
  87.4 8.8 %all-to-all-done = bf16[64,4,128]{2,1,0:T(4,128)(2,1)S(1)} async-done(((bf16[64,4,128]{2,1,0:T(4,128)(2,1)}), bf16[64,4,128]{2,1,0:T(4,128)(2,1)S(1)}, u32[]{:S(2)}, u32[]{:S(2)}) %all-to-all-start) | async-done | bytes 65568 | tf_op jit(solution)/shard_map/while/body/eval_jaxpr/all_to_all | solution.py:65
  96.4 1.3 collective-permute-start
  97.7 4.9 %collective-permute-start.1 = (bf16[128,1]{1,0:T(8,128)(2,1)S(1)}, bf16[128,1]{1,0:T(8,128)(2,1)S(1)}, u32[]{:S(2)}, u32[]{:S(2)}) collective-permute-start(bf16[128,1]{1,0:T(8,128)(2,1)S(1)} %get-tuple-element.171), channel_id=1, source_target_pairs={{0,1},{1,2},{2,3},{4,5},{5,6},{6,7},{8,9},{9,10},{10,11},{12,13},{... | collective-permute-start | bytes 776 | tf_op jit(solution)/shard_map/while/body/eval_jaxpr/ppermute | solution.py:16
  102.8 1.4 collective-permute-done.1
  107.2 5.5 %all-to-all-start = ((bf16[64,4,128]{2,1,0:T(4,128)(2,1)}), bf16[64,4,128]{2,1,0:T(4,128)(2,1)S(1)}, u32[]{:S(2)}, u32[]{:S(2)}) async-start(bf16[64,4,128]{2,1,0:T(4,128)(2,1)} %broadcast_select_fusion.2), calls=%async_computation | async-start | bytes 131072 | tf_op jit(solution)/shard_map/while/body/eval_jaxpr/all_to_all | solution.py:65
  112.7 8.8 %all-to-all-done = bf16[64,4,128]{2,1,0:T(4,128)(2,1)S(1)} async-done(((bf16[64,4,128]{2,1,0:T(4,128)(2,1)}), bf16[64,4,128]{2,1,0:T(4,128)(2,1)S(1)}, u32[]{:S(2)}, u32[]{:S(2)}) %all-to-all-start) | async-done | bytes 65568 | tf_op jit(solution)/shard_map/while/body/eval_jaxpr/all_to_all | solution.py:65
  121.7 1.3 collective-permute-start
  123.0 4.9 %collective-permute-start.1 = (bf16[128,1]{1,0:T(8,128)(2,1)S(1)}, bf16[128,1]{1,0:T(8,128)(2,1)S(1)}, u32[]{:S(2)}, u32[]{:S(2)}) collective-permute-start(bf16[128,1]{1,0:T(8,128)(2,1)S(1)} %get-tuple-element.171), channel_id=1, source_target_pairs={{0,1},{1,2},{2,3},{4,5},{5,6},{6,7},{8,9},{9,10},{10,11},{12,13},{... | collective-permute-start | bytes 776 | tf_op jit(solution)/shard_map/while/body/eval_jaxpr/ppermute | solution.py:16
  128.0 1.4 collective-permute-done.1
  132.4 5.5 %all-to-all-start = ((bf16[64,4,128]{2,1,0:T(4,128)(2,1)}), bf16[64,4,128]{2,1,0:T(4,128)(2,1)S(1)}, u32[]{:S(2)}, u32[]{:S(2)}) async-start(bf16[64,4,128]{2,1,0:T(4,128)(2,1)} %broadcast_select_fusion.2), calls=%async_computation | async-start | bytes 131072 | tf_op jit(solution)/shard_map/while/body/eval_jaxpr/all_to_all | solution.py:65
  137.9 8.8 %all-to-all-done = bf16[64,4,128]{2,1,0:T(4,128)(2,1)S(1)} async-done(((bf16[64,4,128]{2,1,0:T(4,128)(2,1)}), bf16[64,4,128]{2,1,0:T(4,128)(2,1)S(1)}, u32[]{:S(2)}, u32[]{:S(2)}) %all-to-all-start) | async-done | bytes 65568 | tf_op jit(solution)/shard_map/while/body/eval_jaxpr/all_to_all | solution.py:65
  146.9 1.3 collective-permute-start
  148.2 4.9 %collective-permute-start.1 = (bf16[128,1]{1,0:T(8,128)(2,1)S(1)}, bf16[128,1]{1,0:T(8,128)(2,1)S(1)}, u32[]{:S(2)}, u32[]{:S(2)}) collective-permute-start(bf16[128,1]{1,0:T(8,128)(2,1)S(1)} %get-tuple-element.171), channel_id=1, source_target_pairs={{0,1},{1,2},{2,3},{4,5},{5,6},{6,7},{8,9},{9,10},{10,11},{12,13},{... | collective-permute-start | bytes 776 | tf_op jit(solution)/shard_map/while/body/eval_jaxpr/ppermute | solution.py:16
  153.3 1.4 collective-permute-done.1
  154.8 1.3 fusion.52
  157.7 5.5 %all-to-all-start = ((bf16[64,4,128]{2,1,0:T(4,128)(2,1)}), bf16[64,4,128]{2,1,0:T(4,128)(2,1)S(1)}, u32[]{:S(2)}, u32[]{:S(2)}) async-start(bf16[64,4,128]{2,1,0:T(4,128)(2,1)} %broadcast_select_fusion.2), calls=%async_computation | async-start | bytes 131072 | tf_op jit(solution)/shard_map/while/body/eval_jaxpr/all_to_all | solution.py:65
  163.2 8.8 %all-to-all-done = bf16[64,4,128]{2,1,0:T(4,128)(2,1)S(1)} async-done(((bf16[64,4,128]{2,1,0:T(4,128)(2,1)}), bf16[64,4,128]{2,1,0:T(4,128)(2,1)S(1)}, u32[]{:S(2)}, u32[]{:S(2)}) %all-to-all-start) | async-done | bytes 65568 | tf_op jit(solution)/shard_map/while/body/eval_jaxpr/all_to_all | solution.py:65
  172.2 1.3 collective-permute-start
  173.5 4.9 %collective-permute-start.1 = (bf16[128,1]{1,0:T(8,128)(2,1)S(1)}, bf16[128,1]{1,0:T(8,128)(2,1)S(1)}, u32[]{:S(2)}, u32[]{:S(2)}) collective-permute-start(bf16[128,1]{1,0:T(8,128)(2,1)S(1)} %get-tuple-element.171), channel_id=1, source_target_pairs={{0,1},{1,2},{2,3},{4,5},{5,6},{6,7},{8,9},{9,10},{10,11},{12,13},{... | collective-permute-start | bytes 776 | tf_op jit(solution)/shard_map/while/body/eval_jaxpr/ppermute | solution.py:16
  178.5 1.4 collective-permute-done.1
  182.9 5.5 %all-to-all-start = ((bf16[64,4,128]{2,1,0:T(4,128)(2,1)}), bf16[64,4,128]{2,1,0:T(4,128)(2,1)S(1)}, u32[]{:S(2)}, u32[]{:S(2)}) async-start(bf16[64,4,128]{2,1,0:T(4,128)(2,1)} %broadcast_select_fusion.2), calls=%async_computation | async-start | bytes 131072 | tf_op jit(solution)/shard_map/while/body/eval_jaxpr/all_to_all | solution.py:65
  188.5 8.8 %all-to-all-done = bf16[64,4,128]{2,1,0:T(4,128)(2,1)S(1)} async-done(((bf16[64,4,128]{2,1,0:T(4,128)(2,1)}), bf16[64,4,128]{2,1,0:T(4,128)(2,1)S(1)}, u32[]{:S(2)}, u32[]{:S(2)}) %all-to-all-start) | async-done | bytes 65568 | tf_op jit(solution)/shard_map/while/body/eval_jaxpr/all_to_all | solution.py:65
  197.5 1.3 collective-permute-start
  198.7 4.9 %collective-permute-start.1 = (bf16[128,1]{1,0:T(8,128)(2,1)S(1)}, bf16[128,1]{1,0:T(8,128)(2,1)S(1)}, u32[]{:S(2)}, u32[]{:S(2)}) collective-permute-start(bf16[128,1]{1,0:T(8,128)(2,1)S(1)} %get-tuple-element.171), channel_id=1, source_target_pairs={{0,1},{1,2},{2,3},{4,5},{5,6},{6,7},{8,9},{9,10},{10,11},{12,13},{... | collective-permute-start | bytes 776 | tf_op jit(solution)/shard_map/while/body/eval_jaxpr/ppermute | solution.py:16
  203.8 1.4 collective-permute-done.1
  208.2 5.5 %all-to-all-start = ((bf16[64,4,128]{2,1,0:T(4,128)(2,1)}), bf16[64,4,128]{2,1,0:T(4,128)(2,1)S(1)}, u32[]{:S(2)}, u32[]{:S(2)}) async-start(bf16[64,4,128]{2,1,0:T(4,128)(2,1)} %broadcast_select_fusion.2), calls=%async_computation | async-start | bytes 131072 | tf_op jit(solution)/shard_map/while/body/eval_jaxpr/all_to_all | solution.py:65
  213.7 8.8 %all-to-all-done = bf16[64,4,128]{2,1,0:T(4,128)(2,1)S(1)} async-done(((bf16[64,4,128]{2,1,0:T(4,128)(2,1)}), bf16[64,4,128]{2,1,0:T(4,128)(2,1)S(1)}, u32[]{:S(2)}, u32[]{:S(2)}) %all-to-all-start) | async-done | bytes 65568 | tf_op jit(solution)/shard_map/while/body/eval_jaxpr/all_to_all | solution.py:65
  223.9 4.6 fusion.28
  230.1 239.7 %all-reduce.3.cloned.1.call-done = f32[8,4096]{1,0:T(8,128)} async-done(((f32[8,4096]{1,0:T(8,128)}), f32[8,4096]{1,0:T(8,128)}) %all-reduce.3.cloned.1.call-update) | async-done | bytes 131088 | tf_op jit(solution)/shard_map/psum | solution.py:88
  469.8 1.3 constant_dynamic-slice_fusion
  (144 shorter events, 30.9 us)
Async XLA Ops:
  7.2 462.6 %all-reduce.3.cloned.1.call-start = ((), (), s32[]{:S(2)}) async-start(), calls=%async_computation.1 | async-start | bytes 262144 | tf_op jit(solution)/shard_map/psum | solution.py:88
  14.4 6.0 %collective-permute-start = (bf16[128,1]{1,0:T(8,128)(2,1)S(1)}, bf16[128,1]{1,0:T(8,128)(2,1)S(1)}, u32[]{:S(2)}, u32[]{:S(2)}) collective-permute-start(bf16[128,1]{1,0:T(8,128)(2,1)S(1)} %get-tuple-element.170), channel_id=1, source_target_pairs={{1,0},{2,1},{3,2},{5,4},{6,5},{7,6},{9,8},{10,9},{11,10},{13,12},{... | collective-permute-start | bytes 776 | tf_op jit(solution)/shard_map/while/body/eval_jaxpr/ppermute | solution.py:19
  15.7 6.1 %collective-permute-start.1 = (bf16[128,1]{1,0:T(8,128)(2,1)S(1)}, bf16[128,1]{1,0:T(8,128)(2,1)S(1)}, u32[]{:S(2)}, u32[]{:S(2)}) collective-permute-start(bf16[128,1]{1,0:T(8,128)(2,1)S(1)} %get-tuple-element.171), channel_id=1, source_target_pairs={{0,1},{1,2},{2,3},{4,5},{5,6},{6,7},{8,9},{9,10},{10,11},{12,13},{... | collective-permute-start | bytes 776 | tf_op jit(solution)/shard_map/while/body/eval_jaxpr/ppermute | solution.py:16
  24.8 20.9 %all-to-all-start = ((bf16[64,4,128]{2,1,0:T(4,128)(2,1)}), bf16[64,4,128]{2,1,0:T(4,128)(2,1)S(1)}, u32[]{:S(2)}, u32[]{:S(2)}) async-start(bf16[64,4,128]{2,1,0:T(4,128)(2,1)} %broadcast_select_fusion.2), calls=%async_computation | async-start | bytes 131072 | tf_op jit(solution)/shard_map/while/body/eval_jaxpr/all_to_all | solution.py:65
  45.9 6.3 %collective-permute-start = (bf16[128,1]{1,0:T(8,128)(2,1)S(1)}, bf16[128,1]{1,0:T(8,128)(2,1)S(1)}, u32[]{:S(2)}, u32[]{:S(2)}) collective-permute-start(bf16[128,1]{1,0:T(8,128)(2,1)S(1)} %get-tuple-element.170), channel_id=1, source_target_pairs={{1,0},{2,1},{3,2},{5,4},{6,5},{7,6},{9,8},{10,9},{11,10},{13,12},{... | collective-permute-start | bytes 776 | tf_op jit(solution)/shard_map/while/body/eval_jaxpr/ppermute | solution.py:19
  47.2 6.4 %collective-permute-start.1 = (bf16[128,1]{1,0:T(8,128)(2,1)S(1)}, bf16[128,1]{1,0:T(8,128)(2,1)S(1)}, u32[]{:S(2)}, u32[]{:S(2)}) collective-permute-start(bf16[128,1]{1,0:T(8,128)(2,1)S(1)} %get-tuple-element.171), channel_id=1, source_target_pairs={{0,1},{1,2},{2,3},{4,5},{5,6},{6,7},{8,9},{9,10},{10,11},{12,13},{... | collective-permute-start | bytes 776 | tf_op jit(solution)/shard_map/while/body/eval_jaxpr/ppermute | solution.py:16
  56.7 14.4 %all-to-all-start = ((bf16[64,4,128]{2,1,0:T(4,128)(2,1)}), bf16[64,4,128]{2,1,0:T(4,128)(2,1)S(1)}, u32[]{:S(2)}, u32[]{:S(2)}) async-start(bf16[64,4,128]{2,1,0:T(4,128)(2,1)} %broadcast_select_fusion.2), calls=%async_computation | async-start | bytes 131072 | tf_op jit(solution)/shard_map/while/body/eval_jaxpr/all_to_all | solution.py:65
  71.2 6.3 %collective-permute-start = (bf16[128,1]{1,0:T(8,128)(2,1)S(1)}, bf16[128,1]{1,0:T(8,128)(2,1)S(1)}, u32[]{:S(2)}, u32[]{:S(2)}) collective-permute-start(bf16[128,1]{1,0:T(8,128)(2,1)S(1)} %get-tuple-element.170), channel_id=1, source_target_pairs={{1,0},{2,1},{3,2},{5,4},{6,5},{7,6},{9,8},{10,9},{11,10},{13,12},{... | collective-permute-start | bytes 776 | tf_op jit(solution)/shard_map/while/body/eval_jaxpr/ppermute | solution.py:19
  72.5 6.4 %collective-permute-start.1 = (bf16[128,1]{1,0:T(8,128)(2,1)S(1)}, bf16[128,1]{1,0:T(8,128)(2,1)S(1)}, u32[]{:S(2)}, u32[]{:S(2)}) collective-permute-start(bf16[128,1]{1,0:T(8,128)(2,1)S(1)} %get-tuple-element.171), channel_id=1, source_target_pairs={{0,1},{1,2},{2,3},{4,5},{5,6},{6,7},{8,9},{9,10},{10,11},{12,13},{... | collective-permute-start | bytes 776 | tf_op jit(solution)/shard_map/while/body/eval_jaxpr/ppermute | solution.py:16
  81.9 14.4 %all-to-all-start = ((bf16[64,4,128]{2,1,0:T(4,128)(2,1)}), bf16[64,4,128]{2,1,0:T(4,128)(2,1)S(1)}, u32[]{:S(2)}, u32[]{:S(2)}) async-start(bf16[64,4,128]{2,1,0:T(4,128)(2,1)} %broadcast_select_fusion.2), calls=%async_computation | async-start | bytes 131072 | tf_op jit(solution)/shard_map/while/body/eval_jaxpr/all_to_all | solution.py:65
  96.4 6.3 %collective-permute-start = (bf16[128,1]{1,0:T(8,128)(2,1)S(1)}, bf16[128,1]{1,0:T(8,128)(2,1)S(1)}, u32[]{:S(2)}, u32[]{:S(2)}) collective-permute-start(bf16[128,1]{1,0:T(8,128)(2,1)S(1)} %get-tuple-element.170), channel_id=1, source_target_pairs={{1,0},{2,1},{3,2},{5,4},{6,5},{7,6},{9,8},{10,9},{11,10},{13,12},{... | collective-permute-start | bytes 776 | tf_op jit(solution)/shard_map/while/body/eval_jaxpr/ppermute | solution.py:19
  97.7 6.4 %collective-permute-start.1 = (bf16[128,1]{1,0:T(8,128)(2,1)S(1)}, bf16[128,1]{1,0:T(8,128)(2,1)S(1)}, u32[]{:S(2)}, u32[]{:S(2)}) collective-permute-start(bf16[128,1]{1,0:T(8,128)(2,1)S(1)} %get-tuple-element.171), channel_id=1, source_target_pairs={{0,1},{1,2},{2,3},{4,5},{5,6},{6,7},{8,9},{9,10},{10,11},{12,13},{... | collective-permute-start | bytes 776 | tf_op jit(solution)/shard_map/while/body/eval_jaxpr/ppermute | solution.py:16
  107.2 14.4 %all-to-all-start = ((bf16[64,4,128]{2,1,0:T(4,128)(2,1)}), bf16[64,4,128]{2,1,0:T(4,128)(2,1)S(1)}, u32[]{:S(2)}, u32[]{:S(2)}) async-start(bf16[64,4,128]{2,1,0:T(4,128)(2,1)} %broadcast_select_fusion.2), calls=%async_computation | async-start | bytes 131072 | tf_op jit(solution)/shard_map/while/body/eval_jaxpr/all_to_all | solution.py:65
  121.7 6.3 %collective-permute-start = (bf16[128,1]{1,0:T(8,128)(2,1)S(1)}, bf16[128,1]{1,0:T(8,128)(2,1)S(1)}, u32[]{:S(2)}, u32[]{:S(2)}) collective-permute-start(bf16[128,1]{1,0:T(8,128)(2,1)S(1)} %get-tuple-element.170), channel_id=1, source_target_pairs={{1,0},{2,1},{3,2},{5,4},{6,5},{7,6},{9,8},{10,9},{11,10},{13,12},{... | collective-permute-start | bytes 776 | tf_op jit(solution)/shard_map/while/body/eval_jaxpr/ppermute | solution.py:19
  123.0 6.4 %collective-permute-start.1 = (bf16[128,1]{1,0:T(8,128)(2,1)S(1)}, bf16[128,1]{1,0:T(8,128)(2,1)S(1)}, u32[]{:S(2)}, u32[]{:S(2)}) collective-permute-start(bf16[128,1]{1,0:T(8,128)(2,1)S(1)} %get-tuple-element.171), channel_id=1, source_target_pairs={{0,1},{1,2},{2,3},{4,5},{5,6},{6,7},{8,9},{9,10},{10,11},{12,13},{... | collective-permute-start | bytes 776 | tf_op jit(solution)/shard_map/while/body/eval_jaxpr/ppermute | solution.py:16
  132.4 14.4 %all-to-all-start = ((bf16[64,4,128]{2,1,0:T(4,128)(2,1)}), bf16[64,4,128]{2,1,0:T(4,128)(2,1)S(1)}, u32[]{:S(2)}, u32[]{:S(2)}) async-start(bf16[64,4,128]{2,1,0:T(4,128)(2,1)} %broadcast_select_fusion.2), calls=%async_computation | async-start | bytes 131072 | tf_op jit(solution)/shard_map/while/body/eval_jaxpr/all_to_all | solution.py:65
  146.9 6.3 %collective-permute-start = (bf16[128,1]{1,0:T(8,128)(2,1)S(1)}, bf16[128,1]{1,0:T(8,128)(2,1)S(1)}, u32[]{:S(2)}, u32[]{:S(2)}) collective-permute-start(bf16[128,1]{1,0:T(8,128)(2,1)S(1)} %get-tuple-element.170), channel_id=1, source_target_pairs={{1,0},{2,1},{3,2},{5,4},{6,5},{7,6},{9,8},{10,9},{11,10},{13,12},{... | collective-permute-start | bytes 776 | tf_op jit(solution)/shard_map/while/body/eval_jaxpr/ppermute | solution.py:19
  148.2 6.4 %collective-permute-start.1 = (bf16[128,1]{1,0:T(8,128)(2,1)S(1)}, bf16[128,1]{1,0:T(8,128)(2,1)S(1)}, u32[]{:S(2)}, u32[]{:S(2)}) collective-permute-start(bf16[128,1]{1,0:T(8,128)(2,1)S(1)} %get-tuple-element.171), channel_id=1, source_target_pairs={{0,1},{1,2},{2,3},{4,5},{5,6},{6,7},{8,9},{9,10},{10,11},{12,13},{... | collective-permute-start | bytes 776 | tf_op jit(solution)/shard_map/while/body/eval_jaxpr/ppermute | solution.py:16
  157.7 14.4 %all-to-all-start = ((bf16[64,4,128]{2,1,0:T(4,128)(2,1)}), bf16[64,4,128]{2,1,0:T(4,128)(2,1)S(1)}, u32[]{:S(2)}, u32[]{:S(2)}) async-start(bf16[64,4,128]{2,1,0:T(4,128)(2,1)} %broadcast_select_fusion.2), calls=%async_computation | async-start | bytes 131072 | tf_op jit(solution)/shard_map/while/body/eval_jaxpr/all_to_all | solution.py:65
  172.2 6.3 %collective-permute-start = (bf16[128,1]{1,0:T(8,128)(2,1)S(1)}, bf16[128,1]{1,0:T(8,128)(2,1)S(1)}, u32[]{:S(2)}, u32[]{:S(2)}) collective-permute-start(bf16[128,1]{1,0:T(8,128)(2,1)S(1)} %get-tuple-element.170), channel_id=1, source_target_pairs={{1,0},{2,1},{3,2},{5,4},{6,5},{7,6},{9,8},{10,9},{11,10},{13,12},{... | collective-permute-start | bytes 776 | tf_op jit(solution)/shard_map/while/body/eval_jaxpr/ppermute | solution.py:19
  173.5 6.4 %collective-permute-start.1 = (bf16[128,1]{1,0:T(8,128)(2,1)S(1)}, bf16[128,1]{1,0:T(8,128)(2,1)S(1)}, u32[]{:S(2)}, u32[]{:S(2)}) collective-permute-start(bf16[128,1]{1,0:T(8,128)(2,1)S(1)} %get-tuple-element.171), channel_id=1, source_target_pairs={{0,1},{1,2},{2,3},{4,5},{5,6},{6,7},{8,9},{9,10},{10,11},{12,13},{... | collective-permute-start | bytes 776 | tf_op jit(solution)/shard_map/while/body/eval_jaxpr/ppermute | solution.py:16
  182.9 14.4 %all-to-all-start = ((bf16[64,4,128]{2,1,0:T(4,128)(2,1)}), bf16[64,4,128]{2,1,0:T(4,128)(2,1)S(1)}, u32[]{:S(2)}, u32[]{:S(2)}) async-start(bf16[64,4,128]{2,1,0:T(4,128)(2,1)} %broadcast_select_fusion.2), calls=%async_computation | async-start | bytes 131072 | tf_op jit(solution)/shard_map/while/body/eval_jaxpr/all_to_all | solution.py:65
  197.5 6.3 %collective-permute-start = (bf16[128,1]{1,0:T(8,128)(2,1)S(1)}, bf16[128,1]{1,0:T(8,128)(2,1)S(1)}, u32[]{:S(2)}, u32[]{:S(2)}) collective-permute-start(bf16[128,1]{1,0:T(8,128)(2,1)S(1)} %get-tuple-element.170), channel_id=1, source_target_pairs={{1,0},{2,1},{3,2},{5,4},{6,5},{7,6},{9,8},{10,9},{11,10},{13,12},{... | collective-permute-start | bytes 776 | tf_op jit(solution)/shard_map/while/body/eval_jaxpr/ppermute | solution.py:19
  198.7 6.4 %collective-permute-start.1 = (bf16[128,1]{1,0:T(8,128)(2,1)S(1)}, bf16[128,1]{1,0:T(8,128)(2,1)S(1)}, u32[]{:S(2)}, u32[]{:S(2)}) collective-permute-start(bf16[128,1]{1,0:T(8,128)(2,1)S(1)} %get-tuple-element.171), channel_id=1, source_target_pairs={{0,1},{1,2},{2,3},{4,5},{5,6},{6,7},{8,9},{9,10},{10,11},{12,13},{... | collective-permute-start | bytes 776 | tf_op jit(solution)/shard_map/while/body/eval_jaxpr/ppermute | solution.py:16
  208.2 14.4 %all-to-all-start = ((bf16[64,4,128]{2,1,0:T(4,128)(2,1)}), bf16[64,4,128]{2,1,0:T(4,128)(2,1)S(1)}, u32[]{:S(2)}, u32[]{:S(2)}) async-start(bf16[64,4,128]{2,1,0:T(4,128)(2,1)} %broadcast_select_fusion.2), calls=%async_computation | async-start | bytes 131072 | tf_op jit(solution)/shard_map/while/body/eval_jaxpr/all_to_all | solution.py:65
  222.6 248.6 %copy-start = (f32[128,128]{1,0:T(8,128)}, f32[128,128]{1,0:T(8,128)S(1)}, u32[]{:S(2)}) copy-start(f32[128,128]{1,0:T(8,128)S(1)} %get-tuple-element.81) | copy-start | bytes 196612
  222.6 6.0 %copy-start.1 = (s32[1,128,2]{1,2,0:T(2,128)S(1)}, s32[1,128,2]{1,2,0:T(2,128)}, u32[]{:S(2)}) copy-start(s32[1,128,2]{1,2,0:T(2,128)} %param.18) | copy-start | bytes 3076
Sparse Core Ops, SparseCore 0:
  230.2 239.5 all-reduce.2
where the time goes:
time: 480 us; the launch traced here: 478 us
  waiting for transfers between devices  322 us (67%)
  starting transfers between devices  99.5 us (21%)
  matrix products  15.6 us (3%)
  local copies, waits for them, and re-layouts  14.6 us (3%)
  between operations  14.1 us (3%)
  other arithmetic  11.6 us (2%)
    psum x1, waiting for transfers between devices, on_device(): summed = lax.psum(partial_sum, ('tile', 'sec'))  240 us
    all_to_all x8, waiting for transfers between devices, advance_send(): lax.all_to_all(outgoing, 'tile', split_axis=0, concat_axis=0, tiled=True)  70.7 us
    all_to_all x8, starting transfers between devices, advance_send(): lax.all_to_all(outgoing, 'tile', split_axis=0, concat_axis=0, tiled=True)  50.7 us
    ppermute x8, starting transfers between devices, padded_2(): lax.ppermute(lax.slice_in_dim(block, block.shape[dim] - width, None, axis...  38.5 us
    ppermute x8, waiting for transfers between devices, padded_2(): lax.ppermute(lax.slice_in_dim(block, block.shape[dim] - width, None, axis...  11.2 us
    ppermute x8, starting transfers between devices, padded_2(): lax.ppermute(lax.slice_in_dim(block, 0, width, axis=dim), axis, backward)  10.3 us
    dot_general x8, matrix products, cable_update(): jnp.einsum('ci,ji->cj', right_side, inv_cable, precision=lax.Precision.HI...  10.2 us
  transfers between devices with their start and end apart: 25, of which 17 were waited for; matrix products, arithmetic and copies ran while one was open for 0% of the time, Pallas kernels for 0%

commit v1 on v0

--- a/solution.py
+++ b/solution.py
@@ -85,7 +85,7 @@
     )
     partial_sum = jnp.einsum("tskc,skq->tqc", tile_sums, select, precision=lax.Precision.HIGHEST)
     partial_sum = partial_sum.reshape(step_count, tile_total * contact_width)
-    summed = lax.psum(partial_sum, ("tile", "sec"))
+    summed = lax.psum(lax.psum(partial_sum, "tile"), "sec")
     share_width = summed.shape[1] // (tile_count * section_count)
     position = lax.axis_index("tile") * section_count + lax.axis_index("sec")
     probe_share = lax.dynamic_slice_in_dim(summed, position * share_width, share_width, 1)

time: 480 us -> 457 us (0.952)
  waiting for transfers between devices: 322 us -> 299 us
    psum x1 -> x2, waiting for transfers between devices: 240 us -> 217 us  [on_device(): summed = lax.psum(lax.psum(partial_sum, 'tile'), 'sec')]
  transfers between devices with their start and end apart: 25 -> 26, of which waited for: 17 -> 18; matrix products, arithmetic and copies ran while one was open for 0% -> 0% of each run, Pallas kernels for 0% -> 0%
where the time goes in v1:
time: 457 us; the launch traced here: 455 us
  waiting for transfers between devices  299 us (65%)
  starting transfers between devices  99.5 us (22%)
  matrix products  15.6 us (3%)
  local copies, waits for them, and re-layouts  14.6 us (3%)
  between operations  14.1 us (3%)
  other arithmetic  11.6 us (3%)
    psum x2, waiting for transfers between devices, on_device(): summed = lax.psum(lax.psum(partial_sum, 'tile'), 'sec')  217 us
    all_to_all x8, waiting for transfers between devices, advance_send(): lax.all_to_all(outgoing, 'tile', split_axis=0, concat_axis=0, tiled=True)  70.7 us
    all_to_all x8, starting transfers between devices, advance_send(): lax.all_to_all(outgoing, 'tile', split_axis=0, concat_axis=0, tiled=True)  50.6 us
    ppermute x8, starting transfers between devices, padded_2(): lax.ppermute(lax.slice_in_dim(block, block.shape[dim] - width, None, axis...  38.5 us
    ppermute x8, waiting for transfers between devices, padded_2(): lax.ppermute(lax.slice_in_dim(block, block.shape[dim] - width, None, axis...  11.2 us
    ppermute x8, starting transfers between devices, padded_2(): lax.ppermute(lax.slice_in_dim(block, 0, width, axis=dim), axis, backward)  10.3 us
    dot_general x8, matrix products, cable_update(): jnp.einsum('ci,ji->cj', right_side, inv_cable, precision=lax.Precision.HI...  10.2 us
  transfers between devices with their start and end apart: 26, of which 18 were waited for; matrix products, arithmetic and copies ran while one was open for 0% of the time, Pallas kernels for 0%

profile of v1, /device:TPU:8, one launch (start us, length us, event | category | flops | bytes accessed | tf_op | source)
XLA Modules:
  0.0 455.3 jit_solution(10041813562831894835)
XLA Ops:
  14.3 208.3 %while.13 = (s32[]{:T(128)}, f32[128,128]{1,0:T(8,128)S(1)}, bf16[8,64,4,128]{3,2,1,0:T(4,128)(2,1)S(1)}, f32[128,128]{1,0:T(8,128)}, bf16[8,128,128]{2,1,0:T(8,...) while((s32[]{:T(128)}, f32[128,128]{1,0:T(8,128)S(1)}, ...), condition=%wide.region_4.5_spmd, body=%wide.region_3.4_spmd.sunk | while | flops 25629952 | bytes 1626603 | solution.py:68
  14.4 1.3 collective-permute-start
  15.7 4.5 collective-permute-start.1
  20.4 1.4 collective-permute-done.1
  24.8 12.1 %all-to-all-start = ((bf16[64,4,128]{2,1,0:T(4,128)(2,1)}), bf16[64,4,128]{2,1,0:T(4,128)(2,1)S(1)}, u32[]{:S(2)}, u32[]{:S(2)}) async-start(bf16[64,4,128]{2,1,0:T(4,128)(2,1)} %broadcast_select_fusion.2), calls=%async_computation | async-start | bytes 131072 | tf_op jit(solution)/shard_map/while/body/eval_jaxpr/all_to_all | solution.py:65
  36.9 8.8 %all-to-all-done = bf16[64,4,128]{2,1,0:T(4,128)(2,1)S(1)} async-done(((bf16[64,4,128]{2,1,0:T(4,128)(2,1)}), bf16[64,4,128]{2,1,0:T(4,128)(2,1)S(1)}, u32[]{:S(2)}, u32[]{:S(2)}) %all-to-all-start) | async-done | bytes 65568 | tf_op jit(solution)/shard_map/while/body/eval_jaxpr/all_to_all | solution.py:65
  45.9 1.3 collective-permute-start
  47.2 4.9 %collective-permute-start.1 = (bf16[128,1]{1,0:T(8,128)(2,1)S(1)}, bf16[128,1]{1,0:T(8,128)(2,1)S(1)}, u32[]{:S(2)}, u32[]{:S(2)}) collective-permute-start(bf16[128,1]{1,0:T(8,128)(2,1)S(1)} %get-tuple-element.171), channel_id=1, source_target_pairs={{0,1},{1,2},{2,3},{4,5},{5,6},{6,7},{8,9},{9,10},{10,11},{12,13},{... | collective-permute-start | bytes 776 | tf_op jit(solution)/shard_map/while/body/eval_jaxpr/ppermute | solution.py:16
  52.2 1.4 collective-permute-done.1
  56.7 5.5 %all-to-all-start = ((bf16[64,4,128]{2,1,0:T(4,128)(2,1)}), bf16[64,4,128]{2,1,0:T(4,128)(2,1)S(1)}, u32[]{:S(2)}, u32[]{:S(2)}) async-start(bf16[64,4,128]{2,1,0:T(4,128)(2,1)} %broadcast_select_fusion.2), calls=%async_computation | async-start | bytes 131072 | tf_op jit(solution)/shard_map/while/body/eval_jaxpr/all_to_all | solution.py:65
  62.2 8.8 %all-to-all-done = bf16[64,4,128]{2,1,0:T(4,128)(2,1)S(1)} async-done(((bf16[64,4,128]{2,1,0:T(4,128)(2,1)}), bf16[64,4,128]{2,1,0:T(4,128)(2,1)S(1)}, u32[]{:S(2)}, u32[]{:S(2)}) %all-to-all-start) | async-done | bytes 65568 | tf_op jit(solution)/shard_map/while/body/eval_jaxpr/all_to_all | solution.py:65
  71.2 1.3 collective-permute-start
  72.5 4.9 %collective-permute-start.1 = (bf16[128,1]{1,0:T(8,128)(2,1)S(1)}, bf16[128,1]{1,0:T(8,128)(2,1)S(1)}, u32[]{:S(2)}, u32[]{:S(2)}) collective-permute-start(bf16[128,1]{1,0:T(8,128)(2,1)S(1)} %get-tuple-element.171), channel_id=1, source_target_pairs={{0,1},{1,2},{2,3},{4,5},{5,6},{6,7},{8,9},{9,10},{10,11},{12,13},{... | collective-permute-start | bytes 776 | tf_op jit(solution)/shard_map/while/body/eval_jaxpr/ppermute | solution.py:16
  77.5 1.4 collective-permute-done.1
  81.9 5.5 %all-to-all-start = ((bf16[64,4,128]{2,1,0:T(4,128)(2,1)}), bf16[64,4,128]{2,1,0:T(4,128)(2,1)S(1)}, u32[]{:S(2)}, u32[]{:S(2)}) async-start(bf16[64,4,128]{2,1,0:T(4,128)(2,1)} %broadcast_select_fusion.2), calls=%async_computation | async-start | bytes 131072 | tf_op jit(solution)/shard_map/while/body/eval_jaxpr/all_to_all | solution.py:65
  87.4 8.8 %all-to-all-done = bf16[64,4,128]{2,1,0:T(4,128)(2,1)S(1)} async-done(((bf16[64,4,128]{2,1,0:T(4,128)(2,1)}), bf16[64,4,128]{2,1,0:T(4,128)(2,1)S(1)}, u32[]{:S(2)}, u32[]{:S(2)}) %all-to-all-start) | async-done | bytes 65568 | tf_op jit(solution)/shard_map/while/body/eval_jaxpr/all_to_all | solution.py:65
  96.4 1.3 collective-permute-start
  97.7 4.9 %collective-permute-start.1 = (bf16[128,1]{1,0:T(8,128)(2,1)S(1)}, bf16[128,1]{1,0:T(8,128)(2,1)S(1)}, u32[]{:S(2)}, u32[]{:S(2)}) collective-permute-start(bf16[128,1]{1,0:T(8,128)(2,1)S(1)} %get-tuple-element.171), channel_id=1, source_target_pairs={{0,1},{1,2},{2,3},{4,5},{5,6},{6,7},{8,9},{9,10},{10,11},{12,13},{... | collective-permute-start | bytes 776 | tf_op jit(solution)/shard_map/while/body/eval_jaxpr/ppermute | solution.py:16
  102.8 1.4 collective-permute-done.1
  104.3 1.3 fusion.52
  107.2 5.5 %all-to-all-start = ((bf16[64,4,128]{2,1,0:T(4,128)(2,1)}), bf16[64,4,128]{2,1,0:T(4,128)(2,1)S(1)}, u32[]{:S(2)}, u32[]{:S(2)}) async-start(bf16[64,4,128]{2,1,0:T(4,128)(2,1)} %broadcast_select_fusion.2), calls=%async_computation | async-start | bytes 131072 | tf_op jit(solution)/shard_map/while/body/eval_jaxpr/all_to_all | solution.py:65
  112.7 8.8 %all-to-all-done = bf16[64,4,128]{2,1,0:T(4,128)(2,1)S(1)} async-done(((bf16[64,4,128]{2,1,0:T(4,128)(2,1)}), bf16[64,4,128]{2,1,0:T(4,128)(2,1)S(1)}, u32[]{:S(2)}, u32[]{:S(2)}) %all-to-all-start) | async-done | bytes 65568 | tf_op jit(solution)/shard_map/while/body/eval_jaxpr/all_to_all | solution.py:65
  121.7 1.3 collective-permute-start
  123.0 4.8 %collective-permute-start.1 = (bf16[128,1]{1,0:T(8,128)(2,1)S(1)}, bf16[128,1]{1,0:T(8,128)(2,1)S(1)}, u32[]{:S(2)}, u32[]{:S(2)}) collective-permute-start(bf16[128,1]{1,0:T(8,128)(2,1)S(1)} %get-tuple-element.171), channel_id=1, source_target_pairs={{0,1},{1,2},{2,3},{4,5},{5,6},{6,7},{8,9},{9,10},{10,11},{12,13},{... | collective-permute-start | bytes 776 | tf_op jit(solution)/shard_map/while/body/eval_jaxpr/ppermute | solution.py:16
  128.0 1.4 collective-permute-done.1
  132.4 5.5 %all-to-all-start = ((bf16[64,4,128]{2,1,0:T(4,128)(2,1)}), bf16[64,4,128]{2,1,0:T(4,128)(2,1)S(1)}, u32[]{:S(2)}, u32[]{:S(2)}) async-start(bf16[64,4,128]{2,1,0:T(4,128)(2,1)} %broadcast_select_fusion.2), calls=%async_computation | async-start | bytes 131072 | tf_op jit(solution)/shard_map/while/body/eval_jaxpr/all_to_all | solution.py:65
  137.9 8.8 %all-to-all-done = bf16[64,4,128]{2,1,0:T(4,128)(2,1)S(1)} async-done(((bf16[64,4,128]{2,1,0:T(4,128)(2,1)}), bf16[64,4,128]{2,1,0:T(4,128)(2,1)S(1)}, u32[]{:S(2)}, u32[]{:S(2)}) %all-to-all-start) | async-done | bytes 65568 | tf_op jit(solution)/shard_map/while/body/eval_jaxpr/all_to_all | solution.py:65
  146.9 1.3 collective-permute-start
  148.2 4.9 %collective-permute-start.1 = (bf16[128,1]{1,0:T(8,128)(2,1)S(1)}, bf16[128,1]{1,0:T(8,128)(2,1)S(1)}, u32[]{:S(2)}, u32[]{:S(2)}) collective-permute-start(bf16[128,1]{1,0:T(8,128)(2,1)S(1)} %get-tuple-element.171), channel_id=1, source_target_pairs={{0,1},{1,2},{2,3},{4,5},{5,6},{6,7},{8,9},{9,10},{10,11},{12,13},{... | collective-permute-start | bytes 776 | tf_op jit(solution)/shard_map/while/body/eval_jaxpr/ppermute | solution.py:16
  153.3 1.4 collective-permute-done.1
  154.8 1.3 fusion.52
  157.7 5.5 %all-to-all-start = ((bf16[64,4,128]{2,1,0:T(4,128)(2,1)}), bf16[64,4,128]{2,1,0:T(4,128)(2,1)S(1)}, u32[]{:S(2)}, u32[]{:S(2)}) async-start(bf16[64,4,128]{2,1,0:T(4,128)(2,1)} %broadcast_select_fusion.2), calls=%async_computation | async-start | bytes 131072 | tf_op jit(solution)/shard_map/while/body/eval_jaxpr/all_to_all | solution.py:65
  163.2 8.8 %all-to-all-done = bf16[64,4,128]{2,1,0:T(4,128)(2,1)S(1)} async-done(((bf16[64,4,128]{2,1,0:T(4,128)(2,1)}), bf16[64,4,128]{2,1,0:T(4,128)(2,1)S(1)}, u32[]{:S(2)}, u32[]{:S(2)}) %all-to-all-start) | async-done | bytes 65568 | tf_op jit(solution)/shard_map/while/body/eval_jaxpr/all_to_all | solution.py:65
  172.2 1.3 collective-permute-start
  173.5 4.9 %collective-permute-start.1 = (bf16[128,1]{1,0:T(8,128)(2,1)S(1)}, bf16[128,1]{1,0:T(8,128)(2,1)S(1)}, u32[]{:S(2)}, u32[]{:S(2)}) collective-permute-start(bf16[128,1]{1,0:T(8,128)(2,1)S(1)} %get-tuple-element.171), channel_id=1, source_target_pairs={{0,1},{1,2},{2,3},{4,5},{5,6},{6,7},{8,9},{9,10},{10,11},{12,13},{... | collective-permute-start | bytes 776 | tf_op jit(solution)/shard_map/while/body/eval_jaxpr/ppermute | solution.py:16
  178.5 1.4 collective-permute-done.1
  180.0 1.3 fusion.52
  182.9 5.5 %all-to-all-start = ((bf16[64,4,128]{2,1,0:T(4,128)(2,1)}), bf16[64,4,128]{2,1,0:T(4,128)(2,1)S(1)}, u32[]{:S(2)}, u32[]{:S(2)}) async-start(bf16[64,4,128]{2,1,0:T(4,128)(2,1)} %broadcast_select_fusion.2), calls=%async_computation | async-start | bytes 131072 | tf_op jit(solution)/shard_map/while/body/eval_jaxpr/all_to_all | solution.py:65
  188.4 8.8 %all-to-all-done = bf16[64,4,128]{2,1,0:T(4,128)(2,1)S(1)} async-done(((bf16[64,4,128]{2,1,0:T(4,128)(2,1)}), bf16[64,4,128]{2,1,0:T(4,128)(2,1)S(1)}, u32[]{:S(2)}, u32[]{:S(2)}) %all-to-all-start) | async-done | bytes 65568 | tf_op jit(solution)/shard_map/while/body/eval_jaxpr/all_to_all | solution.py:65
  197.4 1.3 collective-permute-start
  198.7 4.8 %collective-permute-start.1 = (bf16[128,1]{1,0:T(8,128)(2,1)S(1)}, bf16[128,1]{1,0:T(8,128)(2,1)S(1)}, u32[]{:S(2)}, u32[]{:S(2)}) collective-permute-start(bf16[128,1]{1,0:T(8,128)(2,1)S(1)} %get-tuple-element.171), channel_id=1, source_target_pairs={{0,1},{1,2},{2,3},{4,5},{5,6},{6,7},{8,9},{9,10},{10,11},{12,13},{... | collective-permute-start | bytes 776 | tf_op jit(solution)/shard_map/while/body/eval_jaxpr/ppermute | solution.py:16
  203.8 1.4 collective-permute-done.1
  208.2 5.5 %all-to-all-start = ((bf16[64,4,128]{2,1,0:T(4,128)(2,1)}), bf16[64,4,128]{2,1,0:T(4,128)(2,1)S(1)}, u32[]{:S(2)}, u32[]{:S(2)}) async-start(bf16[64,4,128]{2,1,0:T(4,128)(2,1)} %broadcast_select_fusion.2), calls=%async_computation | async-start | bytes 131072 | tf_op jit(solution)/shard_map/while/body/eval_jaxpr/all_to_all | solution.py:65
  213.7 8.8 %all-to-all-done = bf16[64,4,128]{2,1,0:T(4,128)(2,1)S(1)} async-done(((bf16[64,4,128]{2,1,0:T(4,128)(2,1)}), bf16[64,4,128]{2,1,0:T(4,128)(2,1)S(1)}, u32[]{:S(2)}, u32[]{:S(2)}) %all-to-all-start) | async-done | bytes 65568 | tf_op jit(solution)/shard_map/while/body/eval_jaxpr/all_to_all | solution.py:65
  223.9 4.6 %fusion.28 = f32[8,128,2,128]{3,0,2,1:T(8,128)S(1)} fusion(bf16[1,128,2,128,128]{4,3,2,1,0:T(8,128)(2,1)} %param.19, bf16[128,8,128]{2,1,0:T(8,128)(2,1)S(1)} %gather_fusion.1, pred[128]{0:T(512)(128)(4,1)S(1)} %compare_and_fusion.1), kind=kOutput, calls=%fused_computation.41 | convolution fusion | flops 67239936 | bytes 9699456 | tf_op jit(solution)/shard_map/tsi,skic->tskc/dot_general | solution.py:82
  230.1 169.8 %all-reduce.4.cloned.1.call-done = f32[8,4096]{1,0:T(8,128)} async-done(((f32[8,4096]{1,0:T(8,128)}), f32[8,4096]{1,0:T(8,128)}) %all-reduce.4.cloned.1.call-update) | async-done | bytes 131088 | tf_op jit(solution)/shard_map/psum | solution.py:88
  400.0 47.1 %all-reduce.6.cloned.1.call-done = f32[8,4096]{1,0:T(8,128)} async-done(((f32[8,4096]{1,0:T(8,128)}), f32[8,4096]{1,0:T(8,128)}) %all-reduce.6.cloned.1.call-update) | async-done | bytes 131088 | tf_op jit(solution)/shard_map/psum | solution.py:88
  447.1 1.3 constant_dynamic-slice_fusion
  (147 shorter events, 32.2 us)
Async XLA Ops:
  7.2 392.8 %all-reduce.4.cloned.1.call-start = ((), (), s32[]{:S(2)}) async-start(), calls=%async_computation.1 | async-start | bytes 262144 | tf_op jit(solution)/shard_map/psum | solution.py:88
  14.4 6.0 %collective-permute-start = (bf16[128,1]{1,0:T(8,128)(2,1)S(1)}, bf16[128,1]{1,0:T(8,128)(2,1)S(1)}, u32[]{:S(2)}, u32[]{:S(2)}) collective-permute-start(bf16[128,1]{1,0:T(8,128)(2,1)S(1)} %get-tuple-element.170), channel_id=1, source_target_pairs={{1,0},{2,1},{3,2},{5,4},{6,5},{7,6},{9,8},{10,9},{11,10},{13,12},{... | collective-permute-start | bytes 776 | tf_op jit(solution)/shard_map/while/body/eval_jaxpr/ppermute | solution.py:19
  15.7 6.1 %collective-permute-start.1 = (bf16[128,1]{1,0:T(8,128)(2,1)S(1)}, bf16[128,1]{1,0:T(8,128)(2,1)S(1)}, u32[]{:S(2)}, u32[]{:S(2)}) collective-permute-start(bf16[128,1]{1,0:T(8,128)(2,1)S(1)} %get-tuple-element.171), channel_id=1, source_target_pairs={{0,1},{1,2},{2,3},{4,5},{5,6},{6,7},{8,9},{9,10},{10,11},{12,13},{... | collective-permute-start | bytes 776 | tf_op jit(solution)/shard_map/while/body/eval_jaxpr/ppermute | solution.py:16
  24.8 20.9 %all-to-all-start = ((bf16[64,4,128]{2,1,0:T(4,128)(2,1)}), bf16[64,4,128]{2,1,0:T(4,128)(2,1)S(1)}, u32[]{:S(2)}, u32[]{:S(2)}) async-start(bf16[64,4,128]{2,1,0:T(4,128)(2,1)} %broadcast_select_fusion.2), calls=%async_computation | async-start | bytes 131072 | tf_op jit(solution)/shard_map/while/body/eval_jaxpr/all_to_all | solution.py:65
  45.9 6.3 %collective-permute-start = (bf16[128,1]{1,0:T(8,128)(2,1)S(1)}, bf16[128,1]{1,0:T(8,128)(2,1)S(1)}, u32[]{:S(2)}, u32[]{:S(2)}) collective-permute-start(bf16[128,1]{1,0:T(8,128)(2,1)S(1)} %get-tuple-element.170), channel_id=1, source_target_pairs={{1,0},{2,1},{3,2},{5,4},{6,5},{7,6},{9,8},{10,9},{11,10},{13,12},{... | collective-permute-start | bytes 776 | tf_op jit(solution)/shard_map/while/body/eval_jaxpr/ppermute | solution.py:19
  47.2 6.4 %collective-permute-start.1 = (bf16[128,1]{1,0:T(8,128)(2,1)S(1)}, bf16[128,1]{1,0:T(8,128)(2,1)S(1)}, u32[]{:S(2)}, u32[]{:S(2)}) collective-permute-start(bf16[128,1]{1,0:T(8,128)(2,1)S(1)} %get-tuple-element.171), channel_id=1, source_target_pairs={{0,1},{1,2},{2,3},{4,5},{5,6},{6,7},{8,9},{9,10},{10,11},{12,13},{... | collective-permute-start | bytes 776 | tf_op jit(solution)/shard_map/while/body/eval_jaxpr/ppermute | solution.py:16
  56.7 14.4 %all-to-all-start = ((bf16[64,4,128]{2,1,0:T(4,128)(2,1)}), bf16[64,4,128]{2,1,0:T(4,128)(2,1)S(1)}, u32[]{:S(2)}, u32[]{:S(2)}) async-start(bf16[64,4,128]{2,1,0:T(4,128)(2,1)} %broadcast_select_fusion.2), calls=%async_computation | async-start | bytes 131072 | tf_op jit(solution)/shard_map/while/body/eval_jaxpr/all_to_all | solution.py:65
  71.2 6.3 %collective-permute-start = (bf16[128,1]{1,0:T(8,128)(2,1)S(1)}, bf16[128,1]{1,0:T(8,128)(2,1)S(1)}, u32[]{:S(2)}, u32[]{:S(2)}) collective-permute-start(bf16[128,1]{1,0:T(8,128)(2,1)S(1)} %get-tuple-element.170), channel_id=1, source_target_pairs={{1,0},{2,1},{3,2},{5,4},{6,5},{7,6},{9,8},{10,9},{11,10},{13,12},{... | collective-permute-start | bytes 776 | tf_op jit(solution)/shard_map/while/body/eval_jaxpr/ppermute | solution.py:19
  72.5 6.4 %collective-permute-start.1 = (bf16[128,1]{1,0:T(8,128)(2,1)S(1)}, bf16[128,1]{1,0:T(8,128)(2,1)S(1)}, u32[]{:S(2)}, u32[]{:S(2)}) collective-permute-start(bf16[128,1]{1,0:T(8,128)(2,1)S(1)} %get-tuple-element.171), channel_id=1, source_target_pairs={{0,1},{1,2},{2,3},{4,5},{5,6},{6,7},{8,9},{9,10},{10,11},{12,13},{... | collective-permute-start | bytes 776 | tf_op jit(solution)/shard_map/while/body/eval_jaxpr/ppermute | solution.py:16
  81.9 14.3 %all-to-all-start = ((bf16[64,4,128]{2,1,0:T(4,128)(2,1)}), bf16[64,4,128]{2,1,0:T(4,128)(2,1)S(1)}, u32[]{:S(2)}, u32[]{:S(2)}) async-start(bf16[64,4,128]{2,1,0:T(4,128)(2,1)} %broadcast_select_fusion.2), calls=%async_computation | async-start | bytes 131072 | tf_op jit(solution)/shard_map/while/body/eval_jaxpr/all_to_all | solution.py:65
  96.4 6.3 %collective-permute-start = (bf16[128,1]{1,0:T(8,128)(2,1)S(1)}, bf16[128,1]{1,0:T(8,128)(2,1)S(1)}, u32[]{:S(2)}, u32[]{:S(2)}) collective-permute-start(bf16[128,1]{1,0:T(8,128)(2,1)S(1)} %get-tuple-element.170), channel_id=1, source_target_pairs={{1,0},{2,1},{3,2},{5,4},{6,5},{7,6},{9,8},{10,9},{11,10},{13,12},{... | collective-permute-start | bytes 776 | tf_op jit(solution)/shard_map/while/body/eval_jaxpr/ppermute | solution.py:19
  97.7 6.4 %collective-permute-start.1 = (bf16[128,1]{1,0:T(8,128)(2,1)S(1)}, bf16[128,1]{1,0:T(8,128)(2,1)S(1)}, u32[]{:S(2)}, u32[]{:S(2)}) collective-permute-start(bf16[128,1]{1,0:T(8,128)(2,1)S(1)} %get-tuple-element.171), channel_id=1, source_target_pairs={{0,1},{1,2},{2,3},{4,5},{5,6},{6,7},{8,9},{9,10},{10,11},{12,13},{... | collective-permute-start | bytes 776 | tf_op jit(solution)/shard_map/while/body/eval_jaxpr/ppermute | solution.py:16
  107.2 14.3 %all-to-all-start = ((bf16[64,4,128]{2,1,0:T(4,128)(2,1)}), bf16[64,4,128]{2,1,0:T(4,128)(2,1)S(1)}, u32[]{:S(2)}, u32[]{:S(2)}) async-start(bf16[64,4,128]{2,1,0:T(4,128)(2,1)} %broadcast_select_fusion.2), calls=%async_computation | async-start | bytes 131072 | tf_op jit(solution)/shard_map/while/body/eval_jaxpr/all_to_all | solution.py:65
  121.7 6.3 %collective-permute-start = (bf16[128,1]{1,0:T(8,128)(2,1)S(1)}, bf16[128,1]{1,0:T(8,128)(2,1)S(1)}, u32[]{:S(2)}, u32[]{:S(2)}) collective-permute-start(bf16[128,1]{1,0:T(8,128)(2,1)S(1)} %get-tuple-element.170), channel_id=1, source_target_pairs={{1,0},{2,1},{3,2},{5,4},{6,5},{7,6},{9,8},{10,9},{11,10},{13,12},{... | collective-permute-start | bytes 776 | tf_op jit(solution)/shard_map/while/body/eval_jaxpr/ppermute | solution.py:19
  123.0 6.4 %collective-permute-start.1 = (bf16[128,1]{1,0:T(8,128)(2,1)S(1)}, bf16[128,1]{1,0:T(8,128)(2,1)S(1)}, u32[]{:S(2)}, u32[]{:S(2)}) collective-permute-start(bf16[128,1]{1,0:T(8,128)(2,1)S(1)} %get-tuple-element.171), channel_id=1, source_target_pairs={{0,1},{1,2},{2,3},{4,5},{5,6},{6,7},{8,9},{9,10},{10,11},{12,13},{... | collective-permute-start | bytes 776 | tf_op jit(solution)/shard_map/while/body/eval_jaxpr/ppermute | solution.py:16
  132.4 14.4 %all-to-all-start = ((bf16[64,4,128]{2,1,0:T(4,128)(2,1)}), bf16[64,4,128]{2,1,0:T(4,128)(2,1)S(1)}, u32[]{:S(2)}, u32[]{:S(2)}) async-start(bf16[64,4,128]{2,1,0:T(4,128)(2,1)} %broadcast_select_fusion.2), calls=%async_computation | async-start | bytes 131072 | tf_op jit(solution)/shard_map/while/body/eval_jaxpr/all_to_all | solution.py:65
  146.9 6.3 %collective-permute-start = (bf16[128,1]{1,0:T(8,128)(2,1)S(1)}, bf16[128,1]{1,0:T(8,128)(2,1)S(1)}, u32[]{:S(2)}, u32[]{:S(2)}) collective-permute-start(bf16[128,1]{1,0:T(8,128)(2,1)S(1)} %get-tuple-element.170), channel_id=1, source_target_pairs={{1,0},{2,1},{3,2},{5,4},{6,5},{7,6},{9,8},{10,9},{11,10},{13,12},{... | collective-permute-start | bytes 776 | tf_op jit(solution)/shard_map/while/body/eval_jaxpr/ppermute | solution.py:19
  148.2 6.4 %collective-permute-start.1 = (bf16[128,1]{1,0:T(8,128)(2,1)S(1)}, bf16[128,1]{1,0:T(8,128)(2,1)S(1)}, u32[]{:S(2)}, u32[]{:S(2)}) collective-permute-start(bf16[128,1]{1,0:T(8,128)(2,1)S(1)} %get-tuple-element.171), channel_id=1, source_target_pairs={{0,1},{1,2},{2,3},{4,5},{5,6},{6,7},{8,9},{9,10},{10,11},{12,13},{... | collective-permute-start | bytes 776 | tf_op jit(solution)/shard_map/while/body/eval_jaxpr/ppermute | solution.py:16
  157.7 14.3 %all-to-all-start = ((bf16[64,4,128]{2,1,0:T(4,128)(2,1)}), bf16[64,4,128]{2,1,0:T(4,128)(2,1)S(1)}, u32[]{:S(2)}, u32[]{:S(2)}) async-start(bf16[64,4,128]{2,1,0:T(4,128)(2,1)} %broadcast_select_fusion.2), calls=%async_computation | async-start | bytes 131072 | tf_op jit(solution)/shard_map/while/body/eval_jaxpr/all_to_all | solution.py:65
  172.2 6.3 %collective-permute-start = (bf16[128,1]{1,0:T(8,128)(2,1)S(1)}, bf16[128,1]{1,0:T(8,128)(2,1)S(1)}, u32[]{:S(2)}, u32[]{:S(2)}) collective-permute-start(bf16[128,1]{1,0:T(8,128)(2,1)S(1)} %get-tuple-element.170), channel_id=1, source_target_pairs={{1,0},{2,1},{3,2},{5,4},{6,5},{7,6},{9,8},{10,9},{11,10},{13,12},{... | collective-permute-start | bytes 776 | tf_op jit(solution)/shard_map/while/body/eval_jaxpr/ppermute | solution.py:19
  173.5 6.4 %collective-permute-start.1 = (bf16[128,1]{1,0:T(8,128)(2,1)S(1)}, bf16[128,1]{1,0:T(8,128)(2,1)S(1)}, u32[]{:S(2)}, u32[]{:S(2)}) collective-permute-start(bf16[128,1]{1,0:T(8,128)(2,1)S(1)} %get-tuple-element.171), channel_id=1, source_target_pairs={{0,1},{1,2},{2,3},{4,5},{5,6},{6,7},{8,9},{9,10},{10,11},{12,13},{... | collective-permute-start | bytes 776 | tf_op jit(solution)/shard_map/while/body/eval_jaxpr/ppermute | solution.py:16
  182.9 14.3 %all-to-all-start = ((bf16[64,4,128]{2,1,0:T(4,128)(2,1)}), bf16[64,4,128]{2,1,0:T(4,128)(2,1)S(1)}, u32[]{:S(2)}, u32[]{:S(2)}) async-start(bf16[64,4,128]{2,1,0:T(4,128)(2,1)} %broadcast_select_fusion.2), calls=%async_computation | async-start | bytes 131072 | tf_op jit(solution)/shard_map/while/body/eval_jaxpr/all_to_all | solution.py:65
  197.4 6.3 %collective-permute-start = (bf16[128,1]{1,0:T(8,128)(2,1)S(1)}, bf16[128,1]{1,0:T(8,128)(2,1)S(1)}, u32[]{:S(2)}, u32[]{:S(2)}) collective-permute-start(bf16[128,1]{1,0:T(8,128)(2,1)S(1)} %get-tuple-element.170), channel_id=1, source_target_pairs={{1,0},{2,1},{3,2},{5,4},{6,5},{7,6},{9,8},{10,9},{11,10},{13,12},{... | collective-permute-start | bytes 776 | tf_op jit(solution)/shard_map/while/body/eval_jaxpr/ppermute | solution.py:19
  198.7 6.4 %collective-permute-start.1 = (bf16[128,1]{1,0:T(8,128)(2,1)S(1)}, bf16[128,1]{1,0:T(8,128)(2,1)S(1)}, u32[]{:S(2)}, u32[]{:S(2)}) collective-permute-start(bf16[128,1]{1,0:T(8,128)(2,1)S(1)} %get-tuple-element.171), channel_id=1, source_target_pairs={{0,1},{1,2},{2,3},{4,5},{5,6},{6,7},{8,9},{9,10},{10,11},{12,13},{... | collective-permute-start | bytes 776 | tf_op jit(solution)/shard_map/while/body/eval_jaxpr/ppermute | solution.py:16
  208.2 14.3 %all-to-all-start = ((bf16[64,4,128]{2,1,0:T(4,128)(2,1)}), bf16[64,4,128]{2,1,0:T(4,128)(2,1)S(1)}, u32[]{:S(2)}, u32[]{:S(2)}) async-start(bf16[64,4,128]{2,1,0:T(4,128)(2,1)} %broadcast_select_fusion.2), calls=%async_computation | async-start | bytes 131072 | tf_op jit(solution)/shard_map/while/body/eval_jaxpr/all_to_all | solution.py:65
  222.6 225.9 %copy-start = (f32[128,128]{1,0:T(8,128)}, f32[128,128]{1,0:T(8,128)S(1)}, u32[]{:S(2)}) copy-start(f32[128,128]{1,0:T(8,128)S(1)} %get-tuple-element.81) | copy-start | bytes 196612
  222.6 6.0 %copy-start.1 = (s32[1,128,2]{1,2,0:T(2,128)S(1)}, s32[1,128,2]{1,2,0:T(2,128)}, u32[]{:S(2)}) copy-start(s32[1,128,2]{1,2,0:T(2,128)} %param.18) | copy-start | bytes 3076
  230.1 217.0 %all-reduce.6.cloned.1.call-start = ((), (), s32[]{:S(2)}) async-start(), calls=%async_computation.2 | async-start | bytes 262144 | tf_op jit(solution)/shard_map/psum | solution.py:88
Sparse Core Ops, SparseCore 0:
  230.2 169.7 all-reduce.3
  402.2 44.8 all-reduce.5
